TPU v7x, 32 devices: a whole 2x2x4 slice. The times are simulated.
32 devices in a mesh: region: 16 (over z, y, x), tm: 2 (over core).
Axes of the slice: x: 2, y: 2, z: 4, core: 2. Of those that a mesh axis runs over, the one named last changes fastest.
Arguments:
- latents: bfloat16 [16, 256, 768], P('region', 'tm')
- output_grad: bfloat16 [16, 256, 768], P('region', 'tm'), may hold values from -6 to 6
- conv_kernel: float32 [4, 768], replicated, may hold values from -1 to 1
- w_query: bfloat16 [768, 768], replicated, may hold values from -0.21875 to 0.21875
- w_key: bfloat16 [768, 768], replicated, may hold values from -0.21875 to 0.21875
- w_value: bfloat16 [768, 768], replicated, may hold values from -0.21875 to 0.21875
- w_out: bfloat16 [768, 768], replicated, may hold values from -0.21875 to 0.21875
- live_counts: int32 [16, 2], P('region', 'tm'), may hold values from 1 to 128, as said below
Outputs:
- input_grad: bfloat16 [16, 256, 768], P('region', 'tm')
Inputs may be any that keep to these rules, and one draw needn't show every extreme that they name: The first live_counts[r, c] of the 128 tokens of region r in span c are valid.
All inputs are finite; a program needn't handle non-finite values.
Results may differ from a plain program's by a relative error of at most 0.018.
The roundings to bfloat16 on the way count: a program that leaves them out, or rounds other values in their place, can miss the bound.
Values may be sent and summed in bfloat16 or wider, within the bound.
A program may use at most 128 MiB of HBM per device.

v0:
```python
import functools
import math

import jax
import jax.numpy as jnp
from jax import lax
from jax.experimental import pallas as pl
from jax.experimental.pallas import tpu as pltpu
from jax.sharding import PartitionSpec as P

H = 12
KW = 4
BLK = 256
NEG = -1e30
bf16 = jnp.bfloat16
f32 = jnp.float32
VM = pl.BlockSpec(memory_space=pltpu.VMEM)
SM = pl.BlockSpec(memory_space=pltpu.SMEM)
ANY = pl.BlockSpec(memory_space=pl.ANY)
MESH = pl.DeviceIdType.MESH


def dot(a, b):
    return jnp.dot(a, b, preferred_element_type=f32)


def dot_t(a, b):
    return lax.dot_general(a, b, (((1,), (1,)), ((), ())), preferred_element_type=f32)


def owner(h, n_reg):
    return (h * n_reg) // H


def head_of(me, n_reg):
    h = (me * H + n_reg - 1) // n_reg
    return h, jnp.logical_and(h < H, owner(h, n_reg) == me)


def enter(n_reg, n_tm, me, mt):
    barrier = pltpu.get_barrier_semaphore()
    for d in range(1, n_reg):
        pl.semaphore_signal(
            barrier,
            inc=1,
            device_id={"region": lax.rem(me + d, n_reg)},
            device_id_type=MESH,
        )
    if n_tm > 1:

        @pl.when(mt > 0)
        def _():
            pl.semaphore_signal(barrier, inc=1, device_id={"tm": mt - 1}, device_id_type=MESH)

        @pl.when(mt < n_tm - 1)
        def _():
            pl.semaphore_signal(barrier, inc=1, device_id={"tm": mt + 1}, device_id_type=MESH)

    def settle():
        peers = n_reg - 1 + jnp.minimum(mt, 1) + jnp.minimum(n_tm - 1 - mt, 1)
        pl.semaphore_wait(barrier, peers)

    return settle


def spread_kernel(
    n_reg, n_tm, lat_ref, og_ref, ck_ref, cnt_ref, wq_ref, wk_ref, wv_ref, wo_ref,
    out_ref, cout_ref,
    wbuf, ext, edge, send, csend, wsem, esem, ssem, rsem, cssem, crsem, lsem,
):
    me = lax.axis_index("region")
    mt = lax.axis_index("tm")
    t, d = lat_ref.shape[1], lat_ref.shape[2]
    hd = d // H
    loads = [
        pltpu.make_async_copy(ref, wbuf.at[i], wsem.at[i])
        for i, ref in enumerate((wo_ref, wq_ref, wk_ref, wv_ref))
    ]
    for load in loads:
        load.start()
    settle = enter(n_reg, n_tm, me, mt)
    count = cnt_ref[0, 0]
    csend[...] = jnp.zeros(csend.shape, jnp.int32) + count
    settle()
    to_next = pltpu.make_async_remote_copy(
        src_ref=lat_ref.at[0, pl.ds(t - 16, 16)],
        dst_ref=edge,
        send_sem=esem.at[0],
        recv_sem=esem.at[1],
        device_id={"tm": jnp.minimum(mt + 1, n_tm - 1)},
        device_id_type=MESH,
    )

    @pl.when(mt < n_tm - 1)
    def _():
        to_next.start()

    ext[8 : 8 + t, :] = lat_ref[0].astype(f32)
    loads[0].wait()
    live = lax.broadcasted_iota(jnp.int32, (t, 1), 0) < count
    g = dot_t(og_ref[0], wbuf[0])
    g = jnp.where(live, g, 0.0).astype(bf16)
    for h in range(H):
        send[h, :, 3 * hd : 4 * hd] = g[:, h * hd : (h + 1) * hd]

    @pl.when(mt == 0)
    def _():
        ext[0:8, :] = jnp.zeros((8, d), f32)

    @pl.when(mt > 0)
    def _():
        to_next.wait_recv()
        ext[0:8, :] = edge[8:16, :].astype(f32)

    hidden = ck_ref[0:1, :] * ext[8 : 8 + t, :]
    for j in range(1, KW):
        hidden = hidden + ck_ref[j : j + 1, :] * ext[8 - j : 8 - j + t, :]
    hidden = hidden.astype(bf16)
    for i in range(3):
        loads[i + 1].wait()
        x = dot(hidden, wbuf[i + 1]).astype(bf16)
        for h in range(H):
            send[h, :, i * hd : (i + 1) * hd] = x[:, h * hd : (h + 1) * hd]

    def copies(i):
        h = lax.rem(me + i, H)
        target = owner(h, n_reg)
        big = pltpu.make_async_remote_copy(
            src_ref=send.at[h],
            dst_ref=out_ref.at[me],
            send_sem=ssem.at[i],
            recv_sem=rsem.at[me],
            device_id={"region": target},
            device_id_type=MESH,
        )
        small = pltpu.make_async_remote_copy(
            src_ref=csend,
            dst_ref=cout_ref.at[me],
            send_sem=cssem.at[i],
            recv_sem=crsem.at[me],
            device_id={"region": target},
            device_id_type=MESH,
        )
        here = pltpu.make_async_copy(send.at[h], out_ref.at[me], lsem.at[0])
        chere = pltpu.make_async_copy(csend, cout_ref.at[me], lsem.at[1])
        return target, big, small, here, chere

    for i in range(H):
        target, big, small, here, chere = copies(i)

        @pl.when(target != me)
        def _():
            small.start()
            big.start()

        @pl.when(target == me)
        def _():
            chere.start()
            here.start()

    for i in range(H):
        target, big, small, here, chere = copies(i)

        @pl.when(target != me)
        def _():
            small.wait_send()
            big.wait_send()

        @pl.when(target == me)
        def _():
            chere.wait()
            here.wait()

    @pl.when(mt < n_tm - 1)
    def _():
        to_next.wait_send()

    _, is_head = head_of(me, n_reg)

    @pl.when(is_head)
    def _():
        for k in range(1, n_reg):
            s = lax.rem(me + k, n_reg)
            pltpu.make_async_copy(csend, cout_ref.at[s], crsem.at[s]).wait()
            pltpu.make_async_copy(send.at[0], out_ref.at[s], rsem.at[s]).wait()


def attend_kernel(
    n_reg, hd, chunk_ref, cnt_ref, out_ref, qk, ka, vg, kt, sbuf, wbuf, dkv, dqp
):
    me = lax.axis_index("region")
    t = chunk_ref.shape[1]
    inv_root = 1.0 / math.sqrt(hd)
    _, is_head = head_of(me, n_reg)

    def lane(rows):
        return lax.broadcasted_iota(jnp.int32, (rows, 2 * hd), 1)

    @pl.when(is_head)
    def _():
        def put(off, rows, a, b, live):
            low = lane(rows) < hd
            bias = jnp.where(jnp.logical_and(lane(rows) == 0, jnp.logical_not(live)), NEG, 0.0)
            qk[pl.ds(off, rows), :] = a
            ka[pl.ds(off, rows), :] = jnp.where(low, bias, a.astype(f32)).astype(bf16)
            vg[pl.ds(off, rows), :] = b

        def pack(r, off):
            off = pl.multiple_of(off, 16)
            count = cnt_ref[r, 0, 0]
            live = lax.broadcasted_iota(jnp.int32, (t, 2 * hd), 0) < count
            put(off, t, chunk_ref[r, :, 0 : 2 * hd], chunk_ref[r, :, 2 * hd : 4 * hd], live)
            return off + (count + 15) // 16 * 16

        total = pl.multiple_of(lax.fori_loop(0, n_reg, pack, 0), 16)
        blank = jnp.zeros((BLK, 2 * hd), bf16)
        put(total, BLK, blank, blank, jnp.zeros((BLK, 2 * hd), jnp.int32) > 0)
        blocks = (total + BLK - 1) // BLK

        def ready(i, c):
            at = pl.multiple_of(i * BLK, BLK)
            kt[i] = ka[pl.ds(at, BLK), :].T[hd:, :]
            dkv[pl.ds(at, BLK), :] = jnp.zeros((BLK, 2 * hd), f32)
            return c

        lax.fori_loop(0, blocks, ready, 0)

        def per_queries(qi, c):
            at = pl.multiple_of(qi * BLK, BLK)
            a = qk[pl.ds(at, BLK), :]
            b = vg[pl.ds(at, BLK), :]
            scaled = a.astype(f32) * inv_root
            low = lane(BLK) < hd
            one = jnp.where(lax.broadcasted_iota(jnp.int32, (hd, BLK), 0) == 0, 1.0, 0.0)
            q_t = scaled.T[0:hd, :]
            qat = jnp.concatenate([one, q_t], axis=0).astype(bf16)
            g_t = b.astype(f32).T[hd:, :]
            gat = jnp.concatenate([g_t, jnp.zeros((hd, BLK), f32)], axis=0).astype(bf16)
            qg = jnp.concatenate(
                [jnp.where(low, scaled, 0.0), jnp.where(low, 0.0, b.astype(f32))], axis=0
            ).astype(bf16)

            def first(ki, carry):
                m, l, dl = carry
                kat = pl.multiple_of(ki * BLK, BLK)
                s = dot(ka[pl.ds(kat, BLK), :], qat)
                w = dot(vg[pl.ds(kat, BLK), :], gat)
                sbuf[ki] = s
                wbuf[ki] = w
                m2 = jnp.maximum(m, jnp.max(s, axis=0, keepdims=True))
                p = jnp.exp(s - m2)
                r = jnp.exp(m - m2)
                l = l * r + jnp.sum(p, axis=0, keepdims=True)
                dl = dl * r + jnp.sum(p * w, axis=0, keepdims=True)
                return m2, l, dl

            m, l, dl = lax.fori_loop(
                0,
                blocks,
                first,
                (jnp.full((1, BLK), NEG, f32), jnp.zeros((1, BLK), f32), jnp.zeros((1, BLK), f32)),
            )
            log_total = m + jnp.log(l)
            delta = dl / l

            def second(ki, dq):
                kat = pl.multiple_of(ki * BLK, BLK)
                att = jnp.exp(sbuf[ki] - log_total)
                ds = (att * (wbuf[ki] - delta)).astype(bf16)
                dkv[pl.ds(kat, BLK), :] += dot(jnp.concatenate([ds, att.astype(bf16)], axis=1), qg)
                return dq + dot(kt[ki], ds)

            dq = lax.fori_loop(0, blocks, second, jnp.zeros((hd, BLK), f32))
            dq = jnp.concatenate([dq * inv_root, jnp.zeros((hd, BLK), f32)], axis=0)
            dqp[pl.ds(at, BLK), :] = dq.T
            return c

        lax.fori_loop(0, blocks, per_queries, 0)

        def unpack(r, off):
            off = pl.multiple_of(off, 16)
            count = cnt_ref[r, 0, 0]
            live = lax.broadcasted_iota(jnp.int32, (t, 2 * hd), 0) < count
            both = jnp.where(live, dkv[pl.ds(off, t), :], 0.0)
            dq = jnp.where(live, dqp[pl.ds(off, t), :], 0.0)
            out_ref[r, 0:t, :] = both.astype(bf16)
            pair = jnp.concatenate([dq[0 : t // 2, 0:hd], dq[t // 2 :, 0:hd]], axis=1)
            out_ref[r, t:, :] = pair.astype(bf16)
            return off + (count + 15) // 16 * 16

        lax.fori_loop(0, n_reg, unpack, 0)


def collect_kernel(
    n_reg, n_tm, part_ref, ck_ref, wq_ref, wk_ref, wv_ref,
    out_ref,
    got, wbuf, xs, ext, wsem, esem, ssem, rsem, lsem,
):
    me = lax.axis_index("region")
    mt = lax.axis_index("tm")
    t, d = out_ref.shape[1], out_ref.shape[2]
    hd = d // H
    loads = [
        pltpu.make_async_copy(ref, wbuf.at[i], wsem.at[i])
        for i, ref in enumerate((wq_ref, wk_ref, wv_ref))
    ]
    for load in loads:
        load.start()
    settle = enter(n_reg, n_tm, me, mt)
    settle()
    head, is_head = head_of(me, n_reg)
    head = jnp.minimum(head, H - 1)

    def away(k):
        r = lax.rem(me + k, n_reg)
        return pltpu.make_async_remote_copy(
            src_ref=part_ref.at[r],
            dst_ref=got.at[head],
            send_sem=ssem.at[k],
            recv_sem=rsem.at[head],
            device_id={"region": r},
            device_id_type=MESH,
        )

    here = pltpu.make_async_copy(part_ref.at[me], got.at[head], lsem)

    @pl.when(is_head)
    def _():
        for k in range(1, n_reg):
            away(k).start()
        here.start()
        here.wait()

    for h in range(H):

        @pl.when(owner(h, n_reg) != me)
        def _():
            pltpu.make_async_copy(part_ref.at[0], got.at[h], rsem.at[h]).wait()

    for h in range(H):
        cols = slice(h * hd, (h + 1) * hd)
        xs[0, 0 : t // 2, cols] = got[h, t:, 0:hd]
        xs[0, t // 2 :, cols] = got[h, t:, hd:]
        xs[1, :, cols] = got[h, 0:t, 0:hd]
        xs[2, :, cols] = got[h, 0:t, hd:]
    for load in loads:
        load.wait()
    side = dot_t(xs[1], wbuf[1]) + dot_t(xs[2], wbuf[2])
    ext[0:t, :] = dot_t(xs[0], wbuf[0]) + side

    to_prev = pltpu.make_async_remote_copy(
        src_ref=ext.at[pl.ds(0, 8)],
        dst_ref=ext.at[pl.ds(t, 8)],
        send_sem=esem.at[0],
        recv_sem=esem.at[1],
        device_id={"tm": jnp.maximum(mt - 1, 0)},
        device_id_type=MESH,
    )

    @pl.when(mt > 0)
    def _():
        to_prev.start()

    @pl.when(is_head)
    def _():
        for k in range(1, n_reg):
            away(k).wait_send()

    @pl.when(mt == n_tm - 1)
    def _():
        ext[t : t + 8, :] = jnp.zeros((8, d), f32)

    @pl.when(mt < n_tm - 1)
    def _():
        to_prev.wait_recv()

    total = ck_ref[0:1, :] * ext[0:t, :]
    for j in range(1, KW):
        total = total + ck_ref[j : j + 1, :] * ext[j : j + t, :]
    out_ref[0] = total.astype(bf16)

    @pl.when(mt > 0)
    def _():
        to_prev.wait_send()


def shards(n_reg, n_tm, latents, output_grad, conv_kernel, w_query, w_key, w_value, w_out, live_counts):
    _, t, d = latents.shape
    hd = d // H
    dma = pltpu.SemaphoreType.DMA
    n = n_reg * t
    blocks = -(-n // BLK)
    chunks, counts = pl.pallas_call(
        functools.partial(spread_kernel, n_reg, n_tm),
        out_shape=(
            jax.ShapeDtypeStruct((n_reg, t, 4 * hd), bf16),
            jax.ShapeDtypeStruct((n_reg, 1, 128), jnp.int32),
        ),
        in_specs=[VM, VM, VM, SM, ANY, ANY, ANY, ANY],
        out_specs=(ANY, ANY),
        scratch_shapes=[
            pltpu.VMEM((4, d, d), bf16),
            pltpu.VMEM((t + 8, d), f32),
            pltpu.VMEM((16, d), bf16),
            pltpu.VMEM((H, t, 4 * hd), bf16),
            pltpu.VMEM((1, 128), jnp.int32),
            dma((4,)),
            dma((2,)),
            dma((H,)),
            dma((n_reg,)),
            dma((H,)),
            dma((n_reg,)),
            dma((2,)),
        ],
        compiler_params=pltpu.CompilerParams(collective_id=0, has_side_effects=True),
        name="spread",
    )(latents, output_grad, conv_kernel, live_counts, w_query, w_key, w_value, w_out)
    part = pl.pallas_call(
        functools.partial(attend_kernel, n_reg, hd),
        out_shape=jax.ShapeDtypeStruct((n_reg, t + t // 2, 2 * hd), bf16),
        in_specs=[VM, SM],
        out_specs=VM,
        scratch_shapes=[
            pltpu.VMEM((n + BLK, 2 * hd), bf16),
            pltpu.VMEM((n + BLK, 2 * hd), bf16),
            pltpu.VMEM((n + BLK, 2 * hd), bf16),
            pltpu.VMEM((blocks, hd, BLK), bf16),
            pltpu.VMEM((blocks, BLK, BLK), f32),
            pltpu.VMEM((blocks, BLK, BLK), f32),
            pltpu.VMEM((n + BLK, 2 * hd), f32),
            pltpu.VMEM((n + BLK, 2 * hd), f32),
        ],
        name="attend",
    )(chunks, counts)
    return pl.pallas_call(
        functools.partial(collect_kernel, n_reg, n_tm),
        out_shape=jax.ShapeDtypeStruct((1, t, d), bf16),
        in_specs=[ANY, VM, ANY, ANY, ANY],
        out_specs=VM,
        scratch_shapes=[
            pltpu.VMEM((H, t + t // 2, 2 * hd), bf16),
            pltpu.VMEM((3, d, d), bf16),
            pltpu.VMEM((3, t, d), bf16),
            pltpu.VMEM((t + 8, d), f32),
            dma((3,)),
            dma((2,)),
            dma((n_reg,)),
            dma((H,)),
            dma,
        ],
        compiler_params=pltpu.CompilerParams(collective_id=1, has_side_effects=True),
        name="collect",
    )(part, conv_kernel, w_query, w_key, w_value)


def solution(mesh):
    shard = P("region", "tm", None)
    in_specs = (shard, shard, P(), P(), P(), P(), P(), P("region", "tm"))
    body = functools.partial(shards, mesh.shape["region"], mesh.shape["tm"])
    return jax.shard_map(body, mesh=mesh, in_specs=in_specs, out_specs=shard, check_vma=False)
```

profile of v0, /device:TPU:15, one launch (start us, length us, event | category | flops | bytes accessed | tf_op | source)
XLA Modules:
  0.0 70.6 jit_solution(2869316953638749396)
XLA Ops:
  0.7 25.2 %spread.1 = (bf16[16,128,256]{2,1,0:T(8,128)(2,1)}, s32[16,1,128]{2,1,0:T(1,128)}) custom-call(bf16[1,128,768]{2,1,0:T(8,128)(2,1)} %lat_ref.1, bf16[1,128,768]{2,1,0:T(8,128)(2,1)} %og_ref.1, f32[4,768]{1,0:T(4,128)} %ck_ref.3, s32[1,1]{1,0:T(1,128)S(6)} %copy.10.cnt_ref, bf16[768,768]{1,0:T(8,128)(2,1)} %wq_ref.3, bf16[768,768]{1,0:T(8,128)(2,1)} %wk_ref.3, ...), custom_call_target="tpu_custom_call" | custom-call | tf_op jit(solution)/shard_map/spread/pallas_call | solution.py:393
  25.8 2.2 %attend.1.part_ref = bf16[16,192,128]{2,1,0:T(8,128)(2,1)} custom-call(bf16[16,128,256]{2,1,0:T(8,128)(2,1)} %get-tuple-element.7.chunk_ref, s32[16,1,128]{2,1,0:T(1,128)} %get-tuple-element.8.cnt_ref), custom_call_target="tpu_custom_call" | custom-call | tf_op jit(solution)/shard_map/attend/pallas_call | solution.py:418
  28.0 41.0 %collect.1 = bf16[1,128,768]{2,1,0:T(8,128)(2,1)} custom-call(bf16[16,192,128]{2,1,0:T(8,128)(2,1)} %attend.1.part_ref, f32[4,768]{1,0:T(4,128)} %ck_ref.3, bf16[768,768]{1,0:T(8,128)(2,1)} %wq_ref.3, bf16[768,768]{1,0:T(8,128)(2,1)} %wk_ref.3, bf16[768,768]{1,0:T(8,128)(2,1)} %wv_ref.3), custom_call_target="tpu_custom_call" | custom-call | tf_op jit(solution)/shard_map/collect/pallas_call | solution.py:435
  69.0 1.6 %copy.11 = bf16[1,128,768]{2,1,0:T(8,128)(2,1)} copy(bf16[1,128,768]{2,1,0:T(8,128)(2,1)} %collect.1) | data formatting | bytes 393216
where the time goes:
time: 71.7 us; the launch traced here: 70.6 us
  Pallas kernels  68.4 us (95%)
  local copies, waits for them, and re-layouts  1.62 us (2%)
    pallas_call x1, Pallas kernels, shards(): pl.pallas_call(functools.partial(collect_kernel, n_reg, n_tm), out_shape=...  41 us
    pallas_call x1, Pallas kernels, shards(): pl.pallas_call(functools.partial(spread_kernel, n_reg, n_tm), out_shape=(...  25.2 us
    pallas_call x1, Pallas kernels, shards(): pl.pallas_call(functools.partial(attend_kernel, n_reg, hd), out_shape=jax...  2.19 us
    unnamed x1, local copies, waits for them, and re-layouts  1.62 us

commit v1 on v0

--- a/solution.py
+++ b/solution.py
@@ -11,6 +11,7 @@
 H = 12
 KW = 4
 BLK = 256
+KBLK = 1024
 NEG = -1e30
 bf16 = jnp.bfloat16
 f32 = jnp.float32
@@ -186,91 +187,102 @@
 
 
 def attend_kernel(
-    n_reg, hd, chunk_ref, cnt_ref, out_ref, qk, ka, vg, kt, sbuf, wbuf, dkv, dqp
+    n_reg, hd, chunk_ref, cnt_ref, out_ref, qk, ka, vg, kt, qt, gt, qg, sbuf, wbuf, dkv, dqp
 ):
     me = lax.axis_index("region")
     t = chunk_ref.shape[1]
     inv_root = 1.0 / math.sqrt(hd)
     _, is_head = head_of(me, n_reg)
+    width = 2 * hd
+    subs = KBLK // BLK
 
     def lane(rows):
-        return lax.broadcasted_iota(jnp.int32, (rows, 2 * hd), 1)
+        return lax.broadcasted_iota(jnp.int32, (rows, width), 1)
 
     @pl.when(is_head)
     def _():
-        def put(off, rows, a, b, live):
-            low = lane(rows) < hd
-            bias = jnp.where(jnp.logical_and(lane(rows) == 0, jnp.logical_not(live)), NEG, 0.0)
-            qk[pl.ds(off, rows), :] = a
-            ka[pl.ds(off, rows), :] = jnp.where(low, bias, a.astype(f32)).astype(bf16)
-            vg[pl.ds(off, rows), :] = b
-
         def pack(r, off):
             off = pl.multiple_of(off, 16)
             count = cnt_ref[r, 0, 0]
-            live = lax.broadcasted_iota(jnp.int32, (t, 2 * hd), 0) < count
-            put(off, t, chunk_ref[r, :, 0 : 2 * hd], chunk_ref[r, :, 2 * hd : 4 * hd], live)
+            a = chunk_ref[r, :, 0:width]
+            dead = lax.broadcasted_iota(jnp.int32, (t, width), 0) >= count
+            bias = jnp.where(jnp.logical_and(lane(t) == 0, dead), NEG, 0.0)
+            qk[pl.ds(off, t), :] = a
+            ka[pl.ds(off, t), :] = jnp.where(lane(t) < hd, bias, a.astype(f32)).astype(bf16)
+            vg[pl.ds(off, t), :] = chunk_ref[r, :, width : 2 * width]
             return off + (count + 15) // 16 * 16
 
-        total = pl.multiple_of(lax.fori_loop(0, n_reg, pack, 0), 16)
-        blank = jnp.zeros((BLK, 2 * hd), bf16)
-        put(total, BLK, blank, blank, jnp.zeros((BLK, 2 * hd), jnp.int32) > 0)
+        total = pl.multiple_of(lax.fori_loop(0, n_reg, pack, 0, unroll=4), 16)
+        blank = jnp.zeros((KBLK, width), bf16)
+        qk[pl.ds(total, KBLK), :] = blank
+        ka[pl.ds(total, KBLK), :] = jnp.where(lane(KBLK) == 0, NEG, 0.0).astype(bf16)
+        vg[pl.ds(total, KBLK), :] = blank
         blocks = (total + BLK - 1) // BLK
+        supers = (total + KBLK - 1) // KBLK
 
         def ready(i, c):
             at = pl.multiple_of(i * BLK, BLK)
-            kt[i] = ka[pl.ds(at, BLK), :].T[hd:, :]
-            dkv[pl.ds(at, BLK), :] = jnp.zeros((BLK, 2 * hd), f32)
+            a = qk[pl.ds(at, BLK), :]
+            b = vg[pl.ds(at, BLK), :]
+            a_t = a.T
+            scaled = (a_t[0:hd, :].astype(f32) * inv_root).astype(bf16)
+            one = jnp.where(lax.broadcasted_iota(jnp.int32, (hd, BLK), 0) == 0, 1.0, 0.0)
+            qt[i] = jnp.concatenate([one.astype(bf16), scaled], axis=0)
+            kt[i] = a_t[hd:, :]
+            gt[i] = jnp.concatenate([b.T[hd:, :], jnp.zeros((hd, BLK), bf16)], axis=0)
+            low = lane(BLK) < hd
+            qg[i, 0:BLK, :] = jnp.where(low, a.astype(f32) * inv_root, 0.0).astype(bf16)
+            qg[i, BLK:, :] = jnp.where(low, 0.0, b.astype(f32)).astype(bf16)
+            dkv[pl.ds(at, BLK), :] = jnp.zeros((BLK, width), f32)
             return c
 
-        lax.fori_loop(0, blocks, ready, 0)
+        lax.fori_loop(0, supers * subs, ready, 0)
+
+        def fold(x, op):
+            return op(x.reshape(BLK // 8, 8, BLK), axis=0)
 
         def per_queries(qi, c):
             at = pl.multiple_of(qi * BLK, BLK)
-            a = qk[pl.ds(at, BLK), :]
-            b = vg[pl.ds(at, BLK), :]
-            scaled = a.astype(f32) * inv_root
-            low = lane(BLK) < hd
-            one = jnp.where(lax.broadcasted_iota(jnp.int32, (hd, BLK), 0) == 0, 1.0, 0.0)
-            q_t = scaled.T[0:hd, :]
-            qat = jnp.concatenate([one, q_t], axis=0).astype(bf16)
-            g_t = b.astype(f32).T[hd:, :]
-            gat = jnp.concatenate([g_t, jnp.zeros((hd, BLK), f32)], axis=0).astype(bf16)
-            qg = jnp.concatenate(
-                [jnp.where(low, scaled, 0.0), jnp.where(low, 0.0, b.astype(f32))], axis=0
-            ).astype(bf16)
-
-            def first(ki, carry):
-                m, l, dl = carry
-                kat = pl.multiple_of(ki * BLK, BLK)
-                s = dot(ka[pl.ds(kat, BLK), :], qat)
-                w = dot(vg[pl.ds(kat, BLK), :], gat)
-                sbuf[ki] = s
-                wbuf[ki] = w
-                m2 = jnp.maximum(m, jnp.max(s, axis=0, keepdims=True))
-                p = jnp.exp(s - m2)
-                r = jnp.exp(m - m2)
-                l = l * r + jnp.sum(p, axis=0, keepdims=True)
-                dl = dl * r + jnp.sum(p * w, axis=0, keepdims=True)
-                return m2, l, dl
-
-            m, l, dl = lax.fori_loop(
-                0,
-                blocks,
-                first,
-                (jnp.full((1, BLK), NEG, f32), jnp.zeros((1, BLK), f32), jnp.zeros((1, BLK), f32)),
-            )
-            log_total = m + jnp.log(l)
-            delta = dl / l
-
-            def second(ki, dq):
-                kat = pl.multiple_of(ki * BLK, BLK)
-                att = jnp.exp(sbuf[ki] - log_total)
-                ds = (att * (wbuf[ki] - delta)).astype(bf16)
-                dkv[pl.ds(kat, BLK), :] += dot(jnp.concatenate([ds, att.astype(bf16)], axis=1), qg)
-                return dq + dot(kt[ki], ds)
-
-            dq = lax.fori_loop(0, blocks, second, jnp.zeros((hd, BLK), f32))
+            qat, gat = qt[qi], gt[qi]
+
+            def first(ki, m):
+                for u in range(subs):
+                    kat = pl.multiple_of(ki * KBLK + u * BLK, BLK)
+                    s = dot(ka[pl.ds(kat, BLK), :], qat)
+                    wbuf[ki * subs + u] = dot(vg[pl.ds(kat, BLK), :], gat)
+                    sbuf[ki * subs + u] = s
+                    m = jnp.maximum(m, fold(s, jnp.max))
+                return m
+
+            m = lax.fori_loop(0, supers, first, jnp.full((8, BLK), NEG, f32))
+            m = jnp.max(m, axis=0, keepdims=True)
+
+            def middle(ki, carry):
+                l, dl = carry
+                for u in range(subs):
+                    p = jnp.exp(sbuf[ki * subs + u] - m)
+                    sbuf[ki * subs + u] = p
+                    l = l + fold(p, jnp.sum)
+                    dl = dl + fold(p * wbuf[ki * subs + u], jnp.sum)
+                return l, dl
+
+            none = jnp.zeros((8, BLK), f32)
+            l, dl = lax.fori_loop(0, supers, middle, (none, none))
+            inv_l = 1.0 / jnp.sum(l, axis=0, keepdims=True)
+            delta = jnp.sum(dl, axis=0, keepdims=True) * inv_l
+            both = qg[qi]
+
+            def last(ki, dq):
+                for u in range(subs):
+                    kat = pl.multiple_of(ki * KBLK + u * BLK, BLK)
+                    att = sbuf[ki * subs + u] * inv_l
+                    ds = (att * (wbuf[ki * subs + u] - delta)).astype(bf16)
+                    pair = jnp.concatenate([ds, att.astype(bf16)], axis=1)
+                    dkv[pl.ds(kat, BLK), :] += dot(pair, both)
+                    dq = dq + dot(kt[ki * subs + u], ds)
+                return dq
+
+            dq = lax.fori_loop(0, supers, last, jnp.zeros((hd, BLK), f32))
             dq = jnp.concatenate([dq * inv_root, jnp.zeros((hd, BLK), f32)], axis=0)
             dqp[pl.ds(at, BLK), :] = dq.T
             return c
@@ -280,7 +292,7 @@
         def unpack(r, off):
             off = pl.multiple_of(off, 16)
             count = cnt_ref[r, 0, 0]
-            live = lax.broadcasted_iota(jnp.int32, (t, 2 * hd), 0) < count
+            live = lax.broadcasted_iota(jnp.int32, (t, width), 0) < count
             both = jnp.where(live, dkv[pl.ds(off, t), :], 0.0)
             dq = jnp.where(live, dqp[pl.ds(off, t), :], 0.0)
             out_ref[r, 0:t, :] = both.astype(bf16)
@@ -288,7 +300,7 @@
             out_ref[r, t:, :] = pair.astype(bf16)
             return off + (count + 15) // 16 * 16
 
-        lax.fori_loop(0, n_reg, unpack, 0)
+        lax.fori_loop(0, n_reg, unpack, 0, unroll=4)
 
 
 def collect_kernel(
@@ -389,7 +401,7 @@
     hd = d // H
     dma = pltpu.SemaphoreType.DMA
     n = n_reg * t
-    blocks = -(-n // BLK)
+    blocks = -(-n // KBLK) * (KBLK // BLK)
     chunks, counts = pl.pallas_call(
         functools.partial(spread_kernel, n_reg, n_tm),
         out_shape=(
@@ -421,14 +433,17 @@
         in_specs=[VM, SM],
         out_specs=VM,
         scratch_shapes=[
-            pltpu.VMEM((n + BLK, 2 * hd), bf16),
-            pltpu.VMEM((n + BLK, 2 * hd), bf16),
-            pltpu.VMEM((n + BLK, 2 * hd), bf16),
+            pltpu.VMEM((n + KBLK, 2 * hd), bf16),
+            pltpu.VMEM((n + KBLK, 2 * hd), bf16),
+            pltpu.VMEM((n + KBLK, 2 * hd), bf16),
             pltpu.VMEM((blocks, hd, BLK), bf16),
+            pltpu.VMEM((blocks, 2 * hd, BLK), bf16),
+            pltpu.VMEM((blocks, 2 * hd, BLK), bf16),
+            pltpu.VMEM((blocks, 2 * BLK, 2 * hd), bf16),
             pltpu.VMEM((blocks, BLK, BLK), f32),
             pltpu.VMEM((blocks, BLK, BLK), f32),
-            pltpu.VMEM((n + BLK, 2 * hd), f32),
-            pltpu.VMEM((n + BLK, 2 * hd), f32),
+            pltpu.VMEM((n + KBLK, 2 * hd), f32),
+            pltpu.VMEM((n + KBLK, 2 * hd), f32),
         ],
         name="attend",
     )(chunks, counts)

time: 71.7 us -> 65.3 us (0.911); the launches traced: 70.6 us -> 65.6 us
  Pallas kernels: 68.4 us -> 63.3 us
    pallas_call x1, Pallas kernels: 41 us -> 35.9 us  [shards(): pl.pallas_call(functools.partial(collect_kernel, n_reg, n_tm), out_shape=...]
where the time goes in v1:
time: 65.3 us; the launch traced here: 65.6 us
  Pallas kernels  63.3 us (97%)
  local copies, waits for them, and re-layouts  1.62 us (2%)
  between operations  0.67 us (1%)
    pallas_call x1, Pallas kernels, shards(): pl.pallas_call(functools.partial(collect_kernel, n_reg, n_tm), out_shape=...  35.9 us
    pallas_call x1, Pallas kernels, shards(): pl.pallas_call(functools.partial(spread_kernel, n_reg, n_tm), out_shape=(...  25.2 us
    pallas_call x1, Pallas kernels, shards(): pl.pallas_call(functools.partial(attend_kernel, n_reg, hd), out_shape=jax...  2.19 us
    unnamed x1, local copies, waits for them, and re-layouts  1.62 us

profile of v1, /device:TPU:15, one launch (start us, length us, event | category | flops | bytes accessed | tf_op | source)
XLA Modules:
  0.0 65.6 jit_solution(10165981846627736506)
XLA Ops:
  0.7 25.2 %spread.1 = (bf16[16,128,256]{2,1,0:T(8,128)(2,1)}, s32[16,1,128]{2,1,0:T(1,128)}) custom-call(bf16[1,128,768]{2,1,0:T(8,128)(2,1)} %lat_ref.1, bf16[1,128,768]{2,1,0:T(8,128)(2,1)} %og_ref.1, f32[4,768]{1,0:T(4,128)} %ck_ref.3, s32[1,1]{1,0:T(1,128)S(6)} %copy.10.cnt_ref, bf16[768,768]{1,0:T(8,128)(2,1)} %wq_ref.3, bf16[768,768]{1,0:T(8,128)(2,1)} %wk_ref.3, ...), custom_call_target="tpu_custom_call" | custom-call | tf_op jit(solution)/shard_map/spread/pallas_call | solution.py:405
  25.8 2.2 %attend.1.part_ref = bf16[16,192,128]{2,1,0:T(8,128)(2,1)} custom-call(bf16[16,128,256]{2,1,0:T(8,128)(2,1)} %get-tuple-element.7.chunk_ref, s32[16,1,128]{2,1,0:T(1,128)} %get-tuple-element.8.cnt_ref), custom_call_target="tpu_custom_call" | custom-call | tf_op jit(solution)/shard_map/attend/pallas_call | solution.py:430
  28.0 35.9 %collect.1 = bf16[1,128,768]{2,1,0:T(8,128)(2,1)} custom-call(bf16[16,192,128]{2,1,0:T(8,128)(2,1)} %attend.1.part_ref, f32[4,768]{1,0:T(4,128)} %ck_ref.3, bf16[768,768]{1,0:T(8,128)(2,1)} %wq_ref.3, bf16[768,768]{1,0:T(8,128)(2,1)} %wk_ref.3, bf16[768,768]{1,0:T(8,128)(2,1)} %wv_ref.3), custom_call_target="tpu_custom_call" | custom-call | tf_op jit(solution)/shard_map/collect/pallas_call | solution.py:450
  64.0 1.6 %copy.11 = bf16[1,128,768]{2,1,0:T(8,128)(2,1)} copy(bf16[1,128,768]{2,1,0:T(8,128)(2,1)} %collect.1) | data formatting | bytes 393216

commit v2 on v1

--- a/solution.py
+++ b/solution.py
@@ -38,36 +38,14 @@
     return h, jnp.logical_and(h < H, owner(h, n_reg) == me)
 
 
-def enter(n_reg, n_tm, me, mt):
-    barrier = pltpu.get_barrier_semaphore()
-    for d in range(1, n_reg):
-        pl.semaphore_signal(
-            barrier,
-            inc=1,
-            device_id={"region": lax.rem(me + d, n_reg)},
-            device_id_type=MESH,
-        )
-    if n_tm > 1:
-
-        @pl.when(mt > 0)
-        def _():
-            pl.semaphore_signal(barrier, inc=1, device_id={"tm": mt - 1}, device_id_type=MESH)
-
-        @pl.when(mt < n_tm - 1)
-        def _():
-            pl.semaphore_signal(barrier, inc=1, device_id={"tm": mt + 1}, device_id_type=MESH)
-
-    def settle():
-        peers = n_reg - 1 + jnp.minimum(mt, 1) + jnp.minimum(n_tm - 1 - mt, 1)
-        pl.semaphore_wait(barrier, peers)
-
-    return settle
+def greet(barrier, **where):
+    pl.semaphore_signal(barrier, inc=1, device_id=where, device_id_type=MESH)
 
 
 def spread_kernel(
     n_reg, n_tm, lat_ref, og_ref, ck_ref, cnt_ref, wq_ref, wk_ref, wv_ref, wo_ref,
     out_ref, cout_ref,
-    wbuf, ext, edge, send, csend, wsem, esem, ssem, rsem, cssem, crsem, lsem,
+    wbuf, ext, edge, send, csend, wsem, esem, ssem, rsem, lsem,
 ):
     me = lax.axis_index("region")
     mt = lax.axis_index("tm")
@@ -79,10 +57,44 @@
     ]
     for load in loads:
         load.start()
-    settle = enter(n_reg, n_tm, me, mt)
+    barrier = pltpu.get_barrier_semaphore()
+    _, is_head = head_of(me, n_reg)
+
+    @pl.when(is_head)
+    def _():
+        for k in range(1, n_reg):
+            greet(barrier, region=lax.rem(me + k, n_reg))
+
+    @pl.when(mt > 0)
+    def _():
+        greet(barrier, tm=jnp.maximum(mt - 1, 0))
+
     count = cnt_ref[0, 0]
     csend[...] = jnp.zeros(csend.shape, jnp.int32) + count
-    settle()
+    ext[0:8, :] = jnp.zeros((8, d), f32)
+    ext[8 : 8 + t, :] = lat_ref[0].astype(f32)
+    loads[0].wait()
+    live = lax.broadcasted_iota(jnp.int32, (t, 1), 0) < count
+    g = dot_t(og_ref[0], wbuf[0])
+    g = jnp.where(live, g, 0.0).astype(bf16)
+    for h in range(H):
+        send[h, :, 3 * hd : 4 * hd] = g[:, h * hd : (h + 1) * hd]
+
+    def project(rows, first):
+        hidden = ck_ref[0:1, :] * ext[8 : 8 + rows, :]
+        for j in range(1, KW):
+            hidden = hidden + ck_ref[j : j + 1, :] * ext[8 - j : 8 - j + rows, :]
+        hidden = hidden.astype(bf16)
+        for i in range(3):
+            if first:
+                loads[i + 1].wait()
+            x = dot(hidden, wbuf[i + 1]).astype(bf16)
+            for h in range(H):
+                send[h, 0:rows, i * hd : (i + 1) * hd] = x[:, h * hd : (h + 1) * hd]
+
+    project(t, True)
+    heads = H - jnp.where(is_head, 1, 0)
+    pl.semaphore_wait(barrier, heads + jnp.minimum(n_tm - 1 - mt, 1))
     to_next = pltpu.make_async_remote_copy(
         src_ref=lat_ref.at[0, pl.ds(t - 16, 16)],
         dst_ref=edge,
@@ -96,94 +108,82 @@
     def _():
         to_next.start()
 
-    ext[8 : 8 + t, :] = lat_ref[0].astype(f32)
-    loads[0].wait()
-    live = lax.broadcasted_iota(jnp.int32, (t, 1), 0) < count
-    g = dot_t(og_ref[0], wbuf[0])
-    g = jnp.where(live, g, 0.0).astype(bf16)
-    for h in range(H):
-        send[h, :, 3 * hd : 4 * hd] = g[:, h * hd : (h + 1) * hd]
-
-    @pl.when(mt == 0)
-    def _():
-        ext[0:8, :] = jnp.zeros((8, d), f32)
-
-    @pl.when(mt > 0)
-    def _():
-        to_next.wait_recv()
-        ext[0:8, :] = edge[8:16, :].astype(f32)
-
-    hidden = ck_ref[0:1, :] * ext[8 : 8 + t, :]
-    for j in range(1, KW):
-        hidden = hidden + ck_ref[j : j + 1, :] * ext[8 - j : 8 - j + t, :]
-    hidden = hidden.astype(bf16)
-    for i in range(3):
-        loads[i + 1].wait()
-        x = dot(hidden, wbuf[i + 1]).astype(bf16)
-        for h in range(H):
-            send[h, :, i * hd : (i + 1) * hd] = x[:, h * hd : (h + 1) * hd]
-
-    def copies(i):
+    parts = (pl.ds(16, t - 16), pl.ds(0, 16))
+
+    def target_of(i):
         h = lax.rem(me + i, H)
-        target = owner(h, n_reg)
-        big = pltpu.make_async_remote_copy(
-            src_ref=send.at[h],
-            dst_ref=out_ref.at[me],
-            send_sem=ssem.at[i],
-            recv_sem=rsem.at[me],
+        return h, owner(h, n_reg)
+
+    def away(i, part):
+        h, target = target_of(i)
+        return pltpu.make_async_remote_copy(
+            src_ref=send.at[h, parts[part]],
+            dst_ref=out_ref.at[me, parts[part]],
+            send_sem=ssem.at[part, i],
+            recv_sem=rsem.at[part, me],
             device_id={"region": target},
             device_id_type=MESH,
         )
-        small = pltpu.make_async_remote_copy(
+
+    def tell(i):
+        return pltpu.make_async_remote_copy(
             src_ref=csend,
             dst_ref=cout_ref.at[me],
-            send_sem=cssem.at[i],
-            recv_sem=crsem.at[me],
-            device_id={"region": target},
+            send_sem=ssem.at[2, i],
+            recv_sem=rsem.at[2, me],
+            device_id={"region": target_of(i)[1]},
             device_id_type=MESH,
         )
-        here = pltpu.make_async_copy(send.at[h], out_ref.at[me], lsem.at[0])
-        chere = pltpu.make_async_copy(csend, cout_ref.at[me], lsem.at[1])
-        return target, big, small, here, chere
+
+    head = jnp.minimum(head_of(me, n_reg)[0], H - 1)
+    here = pltpu.make_async_copy(send.at[head], out_ref.at[me], lsem.at[0])
+    tell_here = pltpu.make_async_copy(csend, cout_ref.at[me], lsem.at[1])
 
     for i in range(H):
-        target, big, small, here, chere = copies(i)
-
-        @pl.when(target != me)
+
+        @pl.when(target_of(i)[1] != me)
         def _():
-            small.start()
-            big.start()
-
-        @pl.when(target == me)
+            away(i, 0).start()
+
+    @pl.when(mt > 0)
+    def _():
+        to_next.wait_recv()
+        ext[0:8, :] = edge[8:16, :].astype(f32)
+        project(16, False)
+
+    for i in range(H):
+
+        @pl.when(target_of(i)[1] != me)
         def _():
-            chere.start()
-            here.start()
+            tell(i).start()
+            away(i, 1).start()
+
+    @pl.when(is_head)
+    def _():
+        tell_here.start()
+        here.start()
+        tell_here.wait()
+        here.wait()
 
     for i in range(H):
-        target, big, small, here, chere = copies(i)
-
-        @pl.when(target != me)
+
+        @pl.when(target_of(i)[1] != me)
         def _():
-            small.wait_send()
-            big.wait_send()
-
-        @pl.when(target == me)
-        def _():
-            chere.wait()
-            here.wait()
+            away(i, 0).wait_send()
+            away(i, 1).wait_send()
+            tell(i).wait_send()
 
     @pl.when(mt < n_tm - 1)
     def _():
         to_next.wait_send()
-
-    _, is_head = head_of(me, n_reg)
 
     @pl.when(is_head)
     def _():
         for k in range(1, n_reg):
             s = lax.rem(me + k, n_reg)
-            pltpu.make_async_copy(csend, cout_ref.at[s], crsem.at[s]).wait()
-            pltpu.make_async_copy(send.at[0], out_ref.at[s], rsem.at[s]).wait()
+            pltpu.make_async_copy(csend, cout_ref.at[s], rsem.at[2, s]).wait()
+            for i, rows in enumerate(parts):
+                pltpu.make_async_copy(send.at[0, rows], out_ref.at[s, rows], rsem.at[i, s]).wait()
 
 
 def attend_kernel(
@@ -318,9 +318,25 @@
     ]
     for load in loads:
         load.start()
-    settle = enter(n_reg, n_tm, me, mt)
-    settle()
+    barrier = pltpu.get_barrier_semaphore()
     head, is_head = head_of(me, n_reg)
+    for i in range(H):
+        target = owner(lax.rem(me + i, H), n_reg)
+
+        @pl.when(target != me)
+        def _():
+            greet(barrier, region=target)
+
+    @pl.when(mt < n_tm - 1)
+    def _():
+        greet(barrier, tm=jnp.minimum(mt + 1, n_tm - 1))
+
+    peers = jnp.where(is_head, n_reg - 1, 0) + jnp.minimum(mt, 1)
+
+    @pl.when(peers > 0)
+    def _():
+        pl.semaphore_wait(barrier, peers)
+
     head = jnp.minimum(head, H - 1)
 
     def away(k):
@@ -418,10 +434,8 @@
             pltpu.VMEM((1, 128), jnp.int32),
             dma((4,)),
             dma((2,)),
-            dma((H,)),
-            dma((n_reg,)),
-            dma((H,)),
-            dma((n_reg,)),
+            dma((3, H)),
+            dma((3, n_reg)),
             dma((2,)),
         ],
         compiler_params=pltpu.CompilerParams(collective_id=0, has_side_effects=True),

time: 65.3 us -> 60.1 us (0.920); the launches traced: 65.6 us -> 59.3 us
  Pallas kernels: 63.3 us -> 57 us
    pallas_call x1, Pallas kernels: 25.2 us -> 21.9 us  [shards(): pl.pallas_call(functools.partial(spread_kernel, n_reg, n_tm), out_shape=(...]
    pallas_call x1, Pallas kernels: 35.9 us -> 33 us  [shards(): pl.pallas_call(functools.partial(collect_kernel, n_reg, n_tm), out_shape=...]
where the time goes in v2:
time: 60.1 us; the launch traced here: 59.3 us
  Pallas kernels  57 us (95%)
  local copies, waits for them, and re-layouts  1.62 us (3%)
  between operations  0.67 us (1%)
    pallas_call x1, Pallas kernels, shards(): pl.pallas_call(functools.partial(collect_kernel, n_reg, n_tm), out_shape=...  33 us
    pallas_call x1, Pallas kernels, shards(): pl.pallas_call(functools.partial(spread_kernel, n_reg, n_tm), out_shape=(...  21.9 us
    pallas_call x1, Pallas kernels, shards(): pl.pallas_call(functools.partial(attend_kernel, n_reg, hd), out_shape=jax...  2.19 us
    unnamed x1, local copies, waits for them, and re-layouts  1.62 us

profile of v2, /device:TPU:15, one launch (start us, length us, event | category | flops | bytes accessed | tf_op | source)
XLA Modules:
  0.0 59.3 jit_solution(16106021361280017672)
XLA Ops:
  0.7 21.9 %spread.1 = (bf16[16,128,256]{2,1,0:T(8,128)(2,1)}, s32[16,1,128]{2,1,0:T(1,128)}) custom-call(bf16[1,128,768]{2,1,0:T(8,128)(2,1)} %lat_ref.1, bf16[1,128,768]{2,1,0:T(8,128)(2,1)} %og_ref.1, f32[4,768]{1,0:T(4,128)} %ck_ref.3, s32[1,1]{1,0:T(1,128)S(6)} %copy.10.cnt_ref, bf16[768,768]{1,0:T(8,128)(2,1)} %wq_ref.3, bf16[768,768]{1,0:T(8,128)(2,1)} %wk_ref.3, ...), custom_call_target="tpu_custom_call" | custom-call | tf_op jit(solution)/shard_map/spread/pallas_call | solution.py:421
  22.5 2.2 %attend.1.part_ref = bf16[16,192,128]{2,1,0:T(8,128)(2,1)} custom-call(bf16[16,128,256]{2,1,0:T(8,128)(2,1)} %get-tuple-element.7.chunk_ref, s32[16,1,128]{2,1,0:T(1,128)} %get-tuple-element.8.cnt_ref), custom_call_target="tpu_custom_call" | custom-call | tf_op jit(solution)/shard_map/attend/pallas_call | solution.py:444
  24.7 33.0 %collect.1 = bf16[1,128,768]{2,1,0:T(8,128)(2,1)} custom-call(bf16[16,192,128]{2,1,0:T(8,128)(2,1)} %attend.1.part_ref, f32[4,768]{1,0:T(4,128)} %ck_ref.3, bf16[768,768]{1,0:T(8,128)(2,1)} %wq_ref.3, bf16[768,768]{1,0:T(8,128)(2,1)} %wk_ref.3, bf16[768,768]{1,0:T(8,128)(2,1)} %wv_ref.3), custom_call_target="tpu_custom_call" | custom-call | tf_op jit(solution)/shard_map/collect/pallas_call | solution.py:464
  57.7 1.6 %copy.11 = bf16[1,128,768]{2,1,0:T(8,128)(2,1)} copy(bf16[1,128,768]{2,1,0:T(8,128)(2,1)} %collect.1) | data formatting | bytes 393216
